TPU v7x, 256 devices: a whole 4x4x8 slice. The times are simulated.
256 devices in a mesh: blk: 32 (over z, x), span: 8 (over y, core).
Axes of the slice: x: 4, y: 4, z: 8, core: 2. Of those that a mesh axis runs over, the one named last changes fastest.
Arguments:
- fluid_adjoint_in: float32 [5, 256, 256, 128], P(None, 'blk', 'span'), may hold values from -4 to 4
- fluid_source: float32 [5, 256, 256, 128], P(None, 'blk', 'span'), may hold values from -24 to 24
- velocity: float32 [3, 256, 256, 128], P(None, 'blk', 'span'), may hold values from 0.1 to 1
- diffusion: float32 [5], replicated, may hold values from 0.5 to 2
- jacobian: float32 [5, 5], replicated, may hold values from -0.4 to 0.4
- wall_coefficient: float32 [32, 256, 128], P('blk', 'span'), may hold values from 0.5 to 2
- metal_costate_prior: float32 [512, 256, 128], P('blk', 'span'), may hold values from -4 to 4
- solid_source: float32 [512, 256, 128], P('blk', 'span'), may hold values from -12 to 12
- conductivity: float32 [512, 256, 128], P('blk', 'span'), may hold values from 0.3 to 3
- tile_owner: int32 [8, 1024, 1], P('span', 'blk'), may hold values from 0 to 31; in each aligned block of 32 rows (0 to 31, 32 to 63, ..., all dimensions but the last counted through in order) at most 3 rows name the same one
- tile_target: int32 [8, 1024], P('span', 'blk'), may hold values from 0 to 31
Outputs:
- fluid_adjoint: float32 [5, 256, 256, 128], P(None, 'blk', 'span')
- solid_adjoint: float32 [512, 256, 128], P('blk', 'span')
- residual_norms: float32 [6], replicated
Inputs may be any that keep to these rules, and one draw needn't show every extreme that they name: `tile_owner`: within the 32 wall tiles of one fluid block (the rows of one device), no owner is named more than 3 times, a bound that some block reaches; every owner is named by some tile.
All inputs are finite; a program needn't handle non-finite values.
Results may differ from a plain program's by a relative error of at most 0.004.
Values sent between devices are 32-bit elements; how exact they have to be, the bound alone decides.
A program may use at most 64 MiB of HBM per device.

v0:
```python
import jax
import jax.numpy as jnp
from jax import lax
from jax.sharding import PartitionSpec as P

FSWEEPS = 4
SSWEEPS = 4
damping_weight = 0.8


def padded(block, sides, width):
    for axis, dim in sides:
        count = lax.axis_size(axis)
        forward = [(i, i + 1) for i in range(count - 1)]
        backward = [(target, source) for source, target in forward]
        low = lax.ppermute(
            lax.slice_in_dim(block, block.shape[dim] - width, None, axis=dim), axis, forward
        )
        high = lax.ppermute(lax.slice_in_dim(block, 0, width, axis=dim), axis, backward)
        block = jnp.concatenate([low, block, high], axis=dim)
    return block


def fluid_operator(bordered_grid_data, velocity, spread, jacobian):
    centre = bordered_grid_data[:, 1:-1, 1:-1, 1:-1]
    x_next = bordered_grid_data[:, 2:, 1:-1, 1:-1]
    y_next = bordered_grid_data[:, 1:-1, 2:, 1:-1]
    z_next = bordered_grid_data[:, 1:-1, 1:-1, 2:]
    beside_all = (
        x_next
        + bordered_grid_data[:, :-2, 1:-1, 1:-1]
        + y_next
        + bordered_grid_data[:, 1:-1, :-2, 1:-1]
        + z_next
        + bordered_grid_data[:, 1:-1, 1:-1, :-2]
    )
    mixing = jnp.einsum("fg,gxyz->fxyz", jacobian, centre, precision=lax.Precision.HIGHEST)
    velocity_sum = velocity[0] + velocity[1] + velocity[2]
    return (
        (6.0 * spread + velocity_sum) * centre
        - spread * beside_all
        - velocity[0] * x_next
        - velocity[1] * y_next
        - velocity[2] * z_next
        + mixing
    )


def face_conductance(kappa_rim):
    centre = kappa_rim[1:-1, 1:-1, 1:-1]
    return (
        0.5 * (centre + kappa_rim[2:, 1:-1, 1:-1]),
        0.5 * (centre + kappa_rim[:-2, 1:-1, 1:-1]),
        0.5 * (centre + kappa_rim[1:-1, 2:, 1:-1]),
        0.5 * (centre + kappa_rim[1:-1, :-2, 1:-1]),
        0.5 * (centre + kappa_rim[1:-1, 1:-1, 2:]),
        0.5 * (centre + kappa_rim[1:-1, 1:-1, :-2]),
    )


def solid_operator(bordered_grid_data, faces, diagonal):
    centre = bordered_grid_data[1:-1, 1:-1, 1:-1]
    flows = (
        faces[0] * bordered_grid_data[2:, 1:-1, 1:-1]
        + faces[1] * bordered_grid_data[:-2, 1:-1, 1:-1]
    )
    flows = (
        flows
        + faces[2] * bordered_grid_data[1:-1, 2:, 1:-1]
        + faces[3] * bordered_grid_data[1:-1, :-2, 1:-1]
    )
    flows = (
        flows
        + faces[4] * bordered_grid_data[1:-1, 1:-1, 2:]
        + faces[5] * bordered_grid_data[1:-1, 1:-1, :-2]
    )
    return diagonal * centre - flows


def pad_depth(array):
    widths = [(0, 0)] * (array.ndim - 1) + [(1, 1)]
    return jnp.pad(array, widths)


def shards(
    fluid_adjoint_in,
    fluid_source,
    velocity,
    diffusion,
    jacobian,
    wall_coefficient,
    metal_costate_prior,
    solid_source,
    conductivity,
    tile_owner,
    tile_target,
):
    highest = lax.Precision.HIGHEST
    spread = diffusion[:, None, None, None]
    fluid_diagonal = (
        6.0 * spread
        + (velocity[0] + velocity[1] + velocity[2])
        + jnp.diagonal(jacobian)[:, None, None, None]
    )
    adjoint = fluid_adjoint_in
    for iteration in range(FSWEEPS):
        bordered_grid_data = padded(adjoint, (("blk", 1), ("span", 2)), 1)
        bordered_grid_data = pad_depth(bordered_grid_data)
        fluid_residual = fluid_source - fluid_operator(
            bordered_grid_data, velocity, spread, jacobian
        )
        adjoint = adjoint + damping_weight * fluid_residual / fluid_diagonal
    fluid_squares = jnp.sum(fluid_residual * fluid_residual, axis=(1, 2, 3))
    wall_flux = wall_coefficient[0] * adjoint[4, 0]
    rows = wall_flux.shape[0]
    blocks = lax.axis_size("blk")
    myself = lax.axis_index("blk")
    owner_local = tile_owner[0, :, 0]
    target_local = tile_target[0, :]
    owners_all, targets_all = (
        lax.all_gather(owner_local, "blk", axis=0, tiled=True),
        lax.all_gather(target_local, "blk", axis=0, tiled=True),
    )
    owner_grid = owners_all.reshape(blocks, rows)
    target_grid = targets_all.reshape(blocks, rows)
    to_myself = owner_grid == myself
    target_hot = target_grid[:, :, None] == jnp.arange(rows, dtype=jnp.int32)[None, None, :]
    placing = (target_hot & to_myself[:, :, None]).astype(jnp.float32).reshape(blocks * rows, rows)
    arrived = lax.all_gather(wall_flux, "blk", axis=0, tiled=True)
    surface = jnp.dot(placing.T, arrived, precision=highest)
    heat_source = solid_source.at[-1].add(surface)
    thermal_state_grid = metal_costate_prior
    kappa_rim = padded(conductivity, (("blk", 0), ("span", 1)), 1)
    kappa_rim = pad_depth(kappa_rim)
    faces = face_conductance(kappa_rim)
    metal_pivot_entries = faces[0] + faces[1] + faces[2] + faces[3] + faces[4] + faces[5]
    for iteration in range(SSWEEPS):
        bordered_grid_data = padded(thermal_state_grid, (("blk", 0), ("span", 1)), 1)
        bordered_grid_data = pad_depth(bordered_grid_data)
        metal_imbalance_grid = heat_source - solid_operator(
            bordered_grid_data, faces, metal_pivot_entries
        )
        thermal_state_grid = (
            thermal_state_grid + damping_weight * metal_imbalance_grid / metal_pivot_entries
        )
    interface_heat_level = thermal_state_grid[-1]
    boundary_patches_finished = lax.all_gather(interface_heat_level, "blk", axis=0, tiled=True)
    output_entries = jnp.take(boundary_patches_finished, owner_local * rows + target_local, axis=0)
    gas_outcome = adjoint.at[4, 0].add(wall_coefficient[0] * output_entries)
    solid_squares = jnp.sum(metal_imbalance_grid * metal_imbalance_grid)[None]
    totals = lax.psum(jnp.concatenate([fluid_squares, solid_squares]), ("blk", "span"))
    every_processor = lax.axis_size("blk") * lax.axis_size("span")
    fluid_cells = float(adjoint.shape[1] * adjoint.shape[2] * adjoint.shape[3] * every_processor)
    solid_cells = float(
        thermal_state_grid.shape[0]
        * thermal_state_grid.shape[1]
        * thermal_state_grid.shape[2]
        * every_processor
    )
    counts = jnp.array([fluid_cells] * 5 + [solid_cells], jnp.float32)
    magnitude_list = jnp.sqrt(totals / counts)
    return (gas_outcome, thermal_state_grid, magnitude_list)


def solution(mesh):
    placed = (
        P(None, "blk", "span", None),
        P(None, "blk", "span", None),
        P(None, "blk", "span", None),
        P(),
        P(),
        P("blk", "span", None),
        P("blk", "span", None),
        P("blk", "span", None),
        P("blk", "span", None),
        P("span", "blk", None),
        P("span", "blk"),
    )
    return jax.shard_map(
        shards,
        mesh=mesh,
        in_specs=placed,
        out_specs=(P(None, "blk", "span", None), P("blk", "span", None), P()),
        check_vma=False,
    )
```

profile of v0, /device:TPU:2, one launch (start us, length us, event | category | flops | bytes accessed | tf_op | source)
XLA Modules:
  0.0 370.5 jit_solution(5415000750408817278)
XLA Ops:
  3.0 3.4 collective-permute-start.1
  6.4 2.4 collective-permute-start
  9.6 3.4 collective-permute-start.17
  13.0 2.4 collective-permute-start.16
  15.5 3.4 collective-permute-start.21
  20.5 26.2 %all-reduce.11 = (s32[1024]{0:T(1024)S(1)}, s32[1024]{0:T(1024)S(1)}) all-reduce(s32[1024]{0:T(1024)S(1)} %bitcast_dynamic-update-slice_fusion.1, s32[1024]{0:T(1024)S(1)} %bitcast_dynamic-update-slice_fusion), channel_id=2, replica_groups=mesh['blk'=32,'span'=8] {'blk'}, use_global_device_ids=true, to_apply=%add.9 | all-reduce | flops 2048 | bytes 16384
  47.4 2.5 collective-permute-start.20
  51.8 3.0 collective-permute-start.3
  56.2 3.7 %collective-permute-start.19 = (f32[18,1,128]{2,1,0:T(1,128)S(1)}, f32[18,1,128]{2,1,0:T(1,128)S(1)}, u32[]{:S(2)}, u32[]{:S(2)}) collective-permute-start(f32[18,1,128]{2,1,0:T(1,128)S(1)} %get-tuple-element.70), channel_id=1, source_target_pairs={{0,1},{1,2},{2,3},{3,4},{4,5},{5,6},{6,7},{8,9},{9,10},{10,11},{11... | collective-permute-start | bytes 27656 | tf_op jit(solution)/shard_map/ppermute | solution.py:16
  60.7 2.7 fusion.10
  65.4 3.9 %collective-permute-start.5 = (f32[5,1,32,128]{3,0,2,1:T(8,128)S(1)}, f32[5,1,32,128]{3,0,2,1:T(8,128)S(1)}, u32[]{:S(2)}, u32[]{:S(2)}) collective-permute-start(f32[5,1,32,128]{3,0,2,1:T(8,128)S(1)} %get-tuple-element.56), channel_id=1, source_target_pairs={{0,8},{8,16},{16,24},{24,32},{32,40},{40,48},{48,56},{56,64},{64,7... | collective-permute-start | bytes 245768 | tf_op jit(solution)/shard_map/ppermute | solution.py:16
  71.0 1.9 collective-permute-done.5
  74.2 3.1 collective-permute-start.7
  79.0 2.2 fusion.11
  83.1 4.2 %collective-permute-start.9 = (f32[5,1,32,128]{3,0,2,1:T(8,128)S(1)}, f32[5,1,32,128]{3,0,2,1:T(8,128)S(1)}, u32[]{:S(2)}, u32[]{:S(2)}) collective-permute-start(f32[5,1,32,128]{3,0,2,1:T(8,128)S(1)} %get-tuple-element.54), channel_id=1, source_target_pairs={{0,8},{8,16},{16,24},{24,32},{32,40},{40,48},{48,56},{56,64},{64,7... | collective-permute-start | bytes 245768 | tf_op jit(solution)/shard_map/ppermute | solution.py:16
  91.8 3.3 collective-permute-start.11
  96.5 5.7 %collective-permute-start.23 = (f32[18,1,128]{2,1,0:T(1,128)S(1)}, f32[18,1,128]{2,1,0:T(1,128)S(1)}, u32[]{:S(2)}, u32[]{:S(2)}) collective-permute-start(f32[18,1,128]{2,1,0:T(1,128)S(1)} %get-tuple-element.72), channel_id=1, source_target_pairs={{0,1},{1,2},{2,3},{3,4},{4,5},{5,6},{6,7},{8,9},{9,10},{10,11},{11... | collective-permute-start | bytes 27656 | tf_op jit(solution)/shard_map/ppermute | solution.py:16
  103.0 2.2 fusion.12
  107.2 3.9 %collective-permute-start.13 = (f32[5,1,32,128]{3,0,2,1:T(8,128)S(1)}, f32[5,1,32,128]{3,0,2,1:T(8,128)S(1)}, u32[]{:S(2)}, u32[]{:S(2)}) collective-permute-start(f32[5,1,32,128]{3,0,2,1:T(8,128)S(1)} %get-tuple-element.52), channel_id=1, source_target_pairs={{0,8},{8,16},{16,24},{24,32},{32,40},{40,48},{48,56},{56,64},{64,7... | collective-permute-start | bytes 245768 | tf_op jit(solution)/shard_map/ppermute | solution.py:16
  112.4 2.3 collective-permute-done.13
  116.2 3.1 collective-permute-start.15
  121.0 2.5 multiply_reduce_fusion
  123.5 59.1 %all_gather.14 = f32[1024,128]{1,0:T(8,128)S(1)} all-gather(f32[32,128]{1,0:T(8,128)S(1)} %bitcast_multiply_fusion), channel_id=1, replica_groups=mesh['blk'=32,'span'=8] {'blk'}, dimensions={0}, use_global_device_ids=true | all-gather | bytes 540672 | tf_op jit(solution)/shard_map/all_gather | solution.py:129
  184.0 1.9 collective-permute-start.24
  186.0 3.9 %collective-permute-start.25 = (f32[1,32,128]{2,1,0:T(8,128)S(1)}, f32[1,32,128]{2,1,0:T(8,128)S(1)}, u32[]{:S(2)}, u32[]{:S(2)}) collective-permute-start(f32[1,32,128]{2,1,0:T(8,128)S(1)} %get-tuple-element.78), channel_id=1, source_target_pairs={{0,8},{8,16},{16,24},{24,32},{32,40},{40,48},{48,56},{56,64},{64,7... | collective-permute-start | bytes 49160 | tf_op jit(solution)/shard_map/ppermute | solution.py:16
  192.9 3.0 collective-permute-start.27
  199.4 3.9 %collective-permute-start.29 = (f32[1,32,128]{2,1,0:T(8,128)S(1)}, f32[1,32,128]{2,1,0:T(8,128)S(1)}, u32[]{:S(2)}, u32[]{:S(2)}) collective-permute-start(f32[1,32,128]{2,1,0:T(8,128)S(1)} %get-tuple-element.76), channel_id=1, source_target_pairs={{0,8},{8,16},{16,24},{24,32},{32,40},{40,48},{48,56},{56,64},{64,7... | collective-permute-start | bytes 49160 | tf_op jit(solution)/shard_map/ppermute | solution.py:16
  206.4 5.1 %collective-permute-start.31 = (f32[18,1,128]{2,1,0:T(1,128)S(1)}, f32[18,1,128]{2,1,0:T(1,128)S(1)}, u32[]{:S(2)}, u32[]{:S(2)}) collective-permute-start(f32[18,1,128]{2,1,0:T(1,128)S(1)} %get-tuple-element.66), channel_id=1, source_target_pairs={{0,1},{1,2},{2,3},{3,4},{4,5},{5,6},{6,7},{8,9},{9,10},{10,11},{11... | collective-permute-start | bytes 27656 | tf_op jit(solution)/shard_map/ppermute | solution.py:16
  215.0 4.2 %collective-permute-start.33 = (f32[1,32,128]{2,1,0:T(8,128)S(1)}, f32[1,32,128]{2,1,0:T(8,128)S(1)}, u32[]{:S(2)}, u32[]{:S(2)}) collective-permute-start(f32[1,32,128]{2,1,0:T(8,128)S(1)} %get-tuple-element.74), channel_id=1, source_target_pairs={{0,8},{8,16},{16,24},{24,32},{32,40},{40,48},{48,56},{56,64},{64,7... | collective-permute-start | bytes 49160 | tf_op jit(solution)/shard_map/ppermute | solution.py:16
  222.0 4.8 %collective-permute-start.35 = (f32[18,1,128]{2,1,0:T(1,128)S(1)}, f32[18,1,128]{2,1,0:T(1,128)S(1)}, u32[]{:S(2)}, u32[]{:S(2)}) collective-permute-start(f32[18,1,128]{2,1,0:T(1,128)S(1)} %get-tuple-element.64), channel_id=1, source_target_pairs={{0,1},{1,2},{2,3},{3,4},{4,5},{5,6},{6,7},{8,9},{9,10},{10,11},{11... | collective-permute-start | bytes 27656 | tf_op jit(solution)/shard_map/ppermute | solution.py:16
  229.6 89.1 %psum.7 = f32[6]{0:T(128)S(1)} all-reduce(f32[6]{0:T(128)S(1)} %pad_maximum_fusion.78), channel_id=1, replica_groups=mesh['blk'=32,'span'=8] {'blk','span'}, use_global_device_ids=true, to_apply=%region_2.3 | all-reduce | flops 6 | bytes 48 | tf_op jit(solution)/shard_map/psum | solution.py:151
  318.9 49.3 %all-gather.2 = f32[1,1024,128]{2,1,0:T(8,128)S(1)} all-gather(f32[1,32,128]{2,1,0:T(8,128)S(1)} %slice.616), channel_id=4, replica_groups=mesh['blk'=32,'span'=8] {'blk'}, dimensions={1}, use_global_device_ids=true | all-gather | bytes 540672 | tf_op jit(solution)/shard_map/all_gather | solution.py:147
  (153 shorter events, 52.3 us)
Async XLA Ops:
  3.0 46.9 %collective-permute-start.1 = (f32[5,1,32,128]{3,0,2,1:T(8,128)}, f32[5,1,32,128]{3,0,2,1:T(8,128)S(1)}, u32[]{:S(2)}, u32[]{:S(2)}) collective-permute-start(f32[5,1,32,128]{3,0,2,1:T(8,128)} %get-tuple-element.59), channel_id=1, source_target_pairs={{0,8},{8,16},{16,24},{24,32},{32,40},{40,48},{48,56},{56,64},{64,7... | collective-permute-start | bytes 245768 | tf_op jit(solution)/shard_map/ppermute | solution.py:16
  6.4 44.0 %collective-permute-start = (f32[5,1,32,128]{3,0,2,1:T(8,128)}, f32[5,1,32,128]{3,0,2,1:T(8,128)S(1)}, u32[]{:S(2)}, u32[]{:S(2)}) collective-permute-start(f32[5,1,32,128]{3,0,2,1:T(8,128)} %get-tuple-element.58), channel_id=1, source_target_pairs={{8,0},{16,8},{24,16},{32,24},{40,32},{48,40},{56,48},{64,56},{72,6... | collective-permute-start | bytes 245768 | tf_op jit(solution)/shard_map/ppermute | solution.py:19
  9.6 37.7 %collective-permute-start.17 = (f32[1,32,128]{2,1,0:T(8,128)S(1)}, f32[1,32,128]{2,1,0:T(8,128)S(1)}, u32[]{:S(2)}, u32[]{:S(2)}) collective-permute-start(f32[1,32,128]{2,1,0:T(8,128)S(1)} %get-tuple-element.80), channel_id=1, source_target_pairs={{0,8},{8,16},{16,24},{24,32},{32,40},{40,48},{48,56},{56,64},{64,7... | collective-permute-start | bytes 49160 | tf_op jit(solution)/shard_map/ppermute | solution.py:16
  13.0 36.9 %collective-permute-start.16 = (f32[1,32,128]{2,1,0:T(8,128)S(1)}, f32[1,32,128]{2,1,0:T(8,128)S(1)}, u32[]{:S(2)}, u32[]{:S(2)}) collective-permute-start(f32[1,32,128]{2,1,0:T(8,128)S(1)} %get-tuple-element.81), channel_id=1, source_target_pairs={{8,0},{16,8},{24,16},{32,24},{40,32},{48,40},{56,48},{64,56},{72,6... | collective-permute-start | bytes 49160 | tf_op jit(solution)/shard_map/ppermute | solution.py:19
  15.5 49.9 %collective-permute-start.21 = (f32[1,32,128]{2,1,0:T(8,128)S(1)}, f32[1,32,128]{2,1,0:T(8,128)S(1)}, u32[]{:S(2)}, u32[]{:S(2)}) collective-permute-start(f32[1,32,128]{2,1,0:T(8,128)S(1)} %get-tuple-element.83), channel_id=1, source_target_pairs={{0,8},{8,16},{16,24},{24,32},{32,40},{40,48},{48,56},{56,64},{64,7... | collective-permute-start | bytes 49160 | tf_op jit(solution)/shard_map/ppermute | solution.py:16
  47.4 39.9 %collective-permute-start.20 = (f32[1,32,128]{2,1,0:T(8,128)S(1)}, f32[1,32,128]{2,1,0:T(8,128)S(1)}, u32[]{:S(2)}, u32[]{:S(2)}) collective-permute-start(f32[1,32,128]{2,1,0:T(8,128)S(1)} %get-tuple-element.82), channel_id=1, source_target_pairs={{8,0},{16,8},{24,16},{32,24},{40,32},{48,40},{56,48},{64,56},{72,6... | collective-permute-start | bytes 49160 | tf_op jit(solution)/shard_map/ppermute | solution.py:19
  50.5 5.7 %collective-permute-start.2 = (f32[5,10,1,128]{3,0,2,1:T(8,128)S(1)}, f32[5,10,1,128]{3,0,2,1:T(8,128)S(1)}, u32[]{:S(2)}, u32[]{:S(2)}) collective-permute-start(f32[5,10,1,128]{3,0,2,1:T(8,128)S(1)} %get-tuple-element.49), channel_id=1, source_target_pairs={{1,0},{2,1},{3,2},{4,3},{5,4},{6,5},{7,6},{9,8},{10,9},{11,10},{12... | collective-permute-start | bytes 76808 | tf_op jit(solution)/shard_map/ppermute | solution.py:19
  51.8 8.1 %collective-permute-start.3 = (f32[5,10,1,128]{3,0,2,1:T(8,128)S(1)}, f32[5,10,1,128]{3,0,2,1:T(8,128)S(1)}, u32[]{:S(2)}, u32[]{:S(2)}) collective-permute-start(f32[5,10,1,128]{3,0,2,1:T(8,128)S(1)} %get-tuple-element.48), channel_id=1, source_target_pairs={{0,1},{1,2},{2,3},{3,4},{4,5},{5,6},{6,7},{8,9},{9,10},{10,11},{11... | collective-permute-start | bytes 76808 | tf_op jit(solution)/shard_map/ppermute | solution.py:16
  54.8 52.3 %collective-permute-start.18 = (f32[18,1,128]{2,1,0:T(1,128)S(1)}, f32[18,1,128]{2,1,0:T(1,128)S(1)}, u32[]{:S(2)}, u32[]{:S(2)}) collective-permute-start(f32[18,1,128]{2,1,0:T(1,128)S(1)} %get-tuple-element.71), channel_id=1, source_target_pairs={{1,0},{2,1},{3,2},{4,3},{5,4},{6,5},{7,6},{9,8},{10,9},{11,10},{12... | collective-permute-start | bytes 27656 | tf_op jit(solution)/shard_map/ppermute | solution.py:19
  56.2 54.9 %collective-permute-start.19 = (f32[18,1,128]{2,1,0:T(1,128)S(1)}, f32[18,1,128]{2,1,0:T(1,128)S(1)}, u32[]{:S(2)}, u32[]{:S(2)}) collective-permute-start(f32[18,1,128]{2,1,0:T(1,128)S(1)} %get-tuple-element.70), channel_id=1, source_target_pairs={{0,1},{1,2},{2,3},{3,4},{4,5},{5,6},{6,7},{8,9},{9,10},{10,11},{11... | collective-permute-start | bytes 27656 | tf_op jit(solution)/shard_map/ppermute | solution.py:16
  63.4 7.5 %collective-permute-start.4 = (f32[5,1,32,128]{3,0,2,1:T(8,128)S(1)}, f32[5,1,32,128]{3,0,2,1:T(8,128)S(1)}, u32[]{:S(2)}, u32[]{:S(2)}) collective-permute-start(f32[5,1,32,128]{3,0,2,1:T(8,128)S(1)} %get-tuple-element.57), channel_id=1, source_target_pairs={{8,0},{16,8},{24,16},{32,24},{40,32},{48,40},{56,48},{64,56},{72,6... | collective-permute-start | bytes 245768 | tf_op jit(solution)/shard_map/ppermute | solution.py:19
  65.4 7.5 %collective-permute-start.5 = (f32[5,1,32,128]{3,0,2,1:T(8,128)S(1)}, f32[5,1,32,128]{3,0,2,1:T(8,128)S(1)}, u32[]{:S(2)}, u32[]{:S(2)}) collective-permute-start(f32[5,1,32,128]{3,0,2,1:T(8,128)S(1)} %get-tuple-element.56), channel_id=1, source_target_pairs={{0,8},{8,16},{16,24},{24,32},{32,40},{40,48},{48,56},{56,64},{64,7... | collective-permute-start | bytes 245768 | tf_op jit(solution)/shard_map/ppermute | solution.py:16
  72.9 4.4 %collective-permute-start.6 = (f32[5,10,1,128]{3,0,2,1:T(8,128)S(1)}, f32[5,10,1,128]{3,0,2,1:T(8,128)S(1)}, u32[]{:S(2)}, u32[]{:S(2)}) collective-permute-start(f32[5,10,1,128]{3,0,2,1:T(8,128)S(1)} %get-tuple-element.47), channel_id=1, source_target_pairs={{1,0},{2,1},{3,2},{4,3},{5,4},{6,5},{7,6},{9,8},{10,9},{11,10},{12... | collective-permute-start | bytes 76808 | tf_op jit(solution)/shard_map/ppermute | solution.py:19
  81.2 7.5 %collective-permute-start.8 = (f32[5,1,32,128]{3,0,2,1:T(8,128)S(1)}, f32[5,1,32,128]{3,0,2,1:T(8,128)S(1)}, u32[]{:S(2)}, u32[]{:S(2)}) collective-permute-start(f32[5,1,32,128]{3,0,2,1:T(8,128)S(1)} %get-tuple-element.55), channel_id=1, source_target_pairs={{8,0},{16,8},{24,16},{32,24},{40,32},{48,40},{56,48},{64,56},{72,6... | collective-permute-start | bytes 245768 | tf_op jit(solution)/shard_map/ppermute | solution.py:19
  83.1 7.4 %collective-permute-start.9 = (f32[5,1,32,128]{3,0,2,1:T(8,128)S(1)}, f32[5,1,32,128]{3,0,2,1:T(8,128)S(1)}, u32[]{:S(2)}, u32[]{:S(2)}) collective-permute-start(f32[5,1,32,128]{3,0,2,1:T(8,128)S(1)} %get-tuple-element.54), channel_id=1, source_target_pairs={{0,8},{8,16},{16,24},{24,32},{32,40},{40,48},{48,56},{56,64},{64,7... | collective-permute-start | bytes 245768 | tf_op jit(solution)/shard_map/ppermute | solution.py:16
  90.5 6.0 %collective-permute-start.10 = (f32[5,10,1,128]{3,0,2,1:T(8,128)S(1)}, f32[5,10,1,128]{3,0,2,1:T(8,128)S(1)}, u32[]{:S(2)}, u32[]{:S(2)}) collective-permute-start(f32[5,10,1,128]{3,0,2,1:T(8,128)S(1)} %get-tuple-element.45), channel_id=1, source_target_pairs={{1,0},{2,1},{3,2},{4,3},{5,4},{6,5},{7,6},{9,8},{10,9},{11,10},{12... | collective-permute-start | bytes 76808 | tf_op jit(solution)/shard_map/ppermute | solution.py:19
  91.8 10.4 %collective-permute-start.11 = (f32[5,10,1,128]{3,0,2,1:T(8,128)S(1)}, f32[5,10,1,128]{3,0,2,1:T(8,128)S(1)}, u32[]{:S(2)}, u32[]{:S(2)}) collective-permute-start(f32[5,10,1,128]{3,0,2,1:T(8,128)S(1)} %get-tuple-element.44), channel_id=1, source_target_pairs={{0,1},{1,2},{2,3},{3,4},{4,5},{5,6},{6,7},{8,9},{9,10},{10,11},{11... | collective-permute-start | bytes 76808 | tf_op jit(solution)/shard_map/ppermute | solution.py:16
  95.2 24.1 %collective-permute-start.22 = (f32[18,1,128]{2,1,0:T(1,128)S(1)}, f32[18,1,128]{2,1,0:T(1,128)S(1)}, u32[]{:S(2)}, u32[]{:S(2)}) collective-permute-start(f32[18,1,128]{2,1,0:T(1,128)S(1)} %get-tuple-element.73), channel_id=1, source_target_pairs={{1,0},{2,1},{3,2},{4,3},{5,4},{6,5},{7,6},{9,8},{10,9},{11,10},{12... | collective-permute-start | bytes 27656 | tf_op jit(solution)/shard_map/ppermute | solution.py:19
  96.5 22.8 %collective-permute-start.23 = (f32[18,1,128]{2,1,0:T(1,128)S(1)}, f32[18,1,128]{2,1,0:T(1,128)S(1)}, u32[]{:S(2)}, u32[]{:S(2)}) collective-permute-start(f32[18,1,128]{2,1,0:T(1,128)S(1)} %get-tuple-element.72), channel_id=1, source_target_pairs={{0,1},{1,2},{2,3},{3,4},{4,5},{5,6},{6,7},{8,9},{9,10},{10,11},{11... | collective-permute-start | bytes 27656 | tf_op jit(solution)/shard_map/ppermute | solution.py:16
  105.2 7.2 %collective-permute-start.12 = (f32[5,1,32,128]{3,0,2,1:T(8,128)S(1)}, f32[5,1,32,128]{3,0,2,1:T(8,128)S(1)}, u32[]{:S(2)}, u32[]{:S(2)}) collective-permute-start(f32[5,1,32,128]{3,0,2,1:T(8,128)S(1)} %get-tuple-element.53), channel_id=1, source_target_pairs={{8,0},{16,8},{24,16},{32,24},{40,32},{48,40},{56,48},{64,56},{72,6... | collective-permute-start | bytes 245768 | tf_op jit(solution)/shard_map/ppermute | solution.py:19
  107.2 7.5 %collective-permute-start.13 = (f32[5,1,32,128]{3,0,2,1:T(8,128)S(1)}, f32[5,1,32,128]{3,0,2,1:T(8,128)S(1)}, u32[]{:S(2)}, u32[]{:S(2)}) collective-permute-start(f32[5,1,32,128]{3,0,2,1:T(8,128)S(1)} %get-tuple-element.52), channel_id=1, source_target_pairs={{0,8},{8,16},{16,24},{24,32},{32,40},{40,48},{48,56},{56,64},{64,7... | collective-permute-start | bytes 245768 | tf_op jit(solution)/shard_map/ppermute | solution.py:16
  114.7 4.9 %collective-permute-start.14 = (f32[5,10,1,128]{3,0,2,1:T(8,128)S(1)}, f32[5,10,1,128]{3,0,2,1:T(8,128)S(1)}, u32[]{:S(2)}, u32[]{:S(2)}) collective-permute-start(f32[5,10,1,128]{3,0,2,1:T(8,128)S(1)} %get-tuple-element.43), channel_id=1, source_target_pairs={{1,0},{2,1},{3,2},{4,3},{5,4},{6,5},{7,6},{9,8},{10,9},{11,10},{12... | collective-permute-start | bytes 76808 | tf_op jit(solution)/shard_map/ppermute | solution.py:19
  184.0 5.9 %collective-permute-start.24 = (f32[1,32,128]{2,1,0:T(8,128)S(1)}, f32[1,32,128]{2,1,0:T(8,128)S(1)}, u32[]{:S(2)}, u32[]{:S(2)}) collective-permute-start(f32[1,32,128]{2,1,0:T(8,128)S(1)} %get-tuple-element.79), channel_id=1, source_target_pairs={{8,0},{16,8},{24,16},{32,24},{40,32},{48,40},{56,48},{64,56},{72,6... | collective-permute-start | bytes 49160 | tf_op jit(solution)/shard_map/ppermute | solution.py:19
  186.0 5.6 %collective-permute-start.25 = (f32[1,32,128]{2,1,0:T(8,128)S(1)}, f32[1,32,128]{2,1,0:T(8,128)S(1)}, u32[]{:S(2)}, u32[]{:S(2)}) collective-permute-start(f32[1,32,128]{2,1,0:T(8,128)S(1)} %get-tuple-element.78), channel_id=1, source_target_pairs={{0,8},{8,16},{16,24},{24,32},{32,40},{40,48},{48,56},{56,64},{64,7... | collective-permute-start | bytes 49160 | tf_op jit(solution)/shard_map/ppermute | solution.py:16
  197.5 5.9 %collective-permute-start.28 = (f32[1,32,128]{2,1,0:T(8,128)S(1)}, f32[1,32,128]{2,1,0:T(8,128)S(1)}, u32[]{:S(2)}, u32[]{:S(2)}) collective-permute-start(f32[1,32,128]{2,1,0:T(8,128)S(1)} %get-tuple-element.77), channel_id=1, source_target_pairs={{8,0},{16,8},{24,16},{32,24},{40,32},{48,40},{56,48},{64,56},{72,6... | collective-permute-start | bytes 49160 | tf_op jit(solution)/shard_map/ppermute | solution.py:19
  199.4 5.6 %collective-permute-start.29 = (f32[1,32,128]{2,1,0:T(8,128)S(1)}, f32[1,32,128]{2,1,0:T(8,128)S(1)}, u32[]{:S(2)}, u32[]{:S(2)}) collective-permute-start(f32[1,32,128]{2,1,0:T(8,128)S(1)} %get-tuple-element.76), channel_id=1, source_target_pairs={{0,8},{8,16},{16,24},{24,32},{32,40},{40,48},{48,56},{56,64},{64,7... | collective-permute-start | bytes 49160 | tf_op jit(solution)/shard_map/ppermute | solution.py:16
  205.1 6.4 %collective-permute-start.30 = (f32[18,1,128]{2,1,0:T(1,128)S(1)}, f32[18,1,128]{2,1,0:T(1,128)S(1)}, u32[]{:S(2)}, u32[]{:S(2)}) collective-permute-start(f32[18,1,128]{2,1,0:T(1,128)S(1)} %get-tuple-element.67), channel_id=1, source_target_pairs={{1,0},{2,1},{3,2},{4,3},{5,4},{6,5},{7,6},{9,8},{10,9},{11,10},{12... | collective-permute-start | bytes 27656 | tf_op jit(solution)/shard_map/ppermute | solution.py:19
  206.4 5.9 %collective-permute-start.31 = (f32[18,1,128]{2,1,0:T(1,128)S(1)}, f32[18,1,128]{2,1,0:T(1,128)S(1)}, u32[]{:S(2)}, u32[]{:S(2)}) collective-permute-start(f32[18,1,128]{2,1,0:T(1,128)S(1)} %get-tuple-element.66), channel_id=1, source_target_pairs={{0,1},{1,2},{2,3},{3,4},{4,5},{5,6},{6,7},{8,9},{9,10},{10,11},{11... | collective-permute-start | bytes 27656 | tf_op jit(solution)/shard_map/ppermute | solution.py:16
  213.1 6.2 %collective-permute-start.32 = (f32[1,32,128]{2,1,0:T(8,128)S(1)}, f32[1,32,128]{2,1,0:T(8,128)S(1)}, u32[]{:S(2)}, u32[]{:S(2)}) collective-permute-start(f32[1,32,128]{2,1,0:T(8,128)S(1)} %get-tuple-element.75), channel_id=1, source_target_pairs={{8,0},{16,8},{24,16},{32,24},{40,32},{48,40},{56,48},{64,56},{72,6... | collective-permute-start | bytes 49160 | tf_op jit(solution)/shard_map/ppermute | solution.py:19
  215.0 5.6 %collective-permute-start.33 = (f32[1,32,128]{2,1,0:T(8,128)S(1)}, f32[1,32,128]{2,1,0:T(8,128)S(1)}, u32[]{:S(2)}, u32[]{:S(2)}) collective-permute-start(f32[1,32,128]{2,1,0:T(8,128)S(1)} %get-tuple-element.74), channel_id=1, source_target_pairs={{0,8},{8,16},{16,24},{24,32},{32,40},{40,48},{48,56},{56,64},{64,7... | collective-permute-start | bytes 49160 | tf_op jit(solution)/shard_map/ppermute | solution.py:16
  220.7 6.1 %collective-permute-start.34 = (f32[18,1,128]{2,1,0:T(1,128)S(1)}, f32[18,1,128]{2,1,0:T(1,128)S(1)}, u32[]{:S(2)}, u32[]{:S(2)}) collective-permute-start(f32[18,1,128]{2,1,0:T(1,128)S(1)} %get-tuple-element.65), channel_id=1, source_target_pairs={{1,0},{2,1},{3,2},{4,3},{5,4},{6,5},{7,6},{9,8},{10,9},{11,10},{12... | collective-permute-start | bytes 27656 | tf_op jit(solution)/shard_map/ppermute | solution.py:19
  222.0 5.6 %collective-permute-start.35 = (f32[18,1,128]{2,1,0:T(1,128)S(1)}, f32[18,1,128]{2,1,0:T(1,128)S(1)}, u32[]{:S(2)}, u32[]{:S(2)}) collective-permute-start(f32[18,1,128]{2,1,0:T(1,128)S(1)} %get-tuple-element.64), channel_id=1, source_target_pairs={{0,1},{1,2},{2,3},{3,4},{4,5},{5,6},{6,7},{8,9},{9,10},{10,11},{11... | collective-permute-start | bytes 27656 | tf_op jit(solution)/shard_map/ppermute | solution.py:16
  (24 other events, 808.0 us)
where the time goes:
time: 372 us; the launch traced here: 370 us
  blocking collectives  224 us (60%)
  starting transfers between devices  99.9 us (27%)
  waiting for transfers between devices  18.5 us (5%)
  matrix products  10.4 us (3%)
  other arithmetic  8.88 us (2%)
  local copies, waits for them, and re-layouts  6.83 us (2%)
    psum x1, blocking collectives, shards(): lax.psum(jnp.concatenate([fluid_squares, solid_squares]), ('blk', 'span'))  89.1 us
    ppermute x18, starting transfers between devices, padded(): lax.ppermute(lax.slice_in_dim(block, block.shape[dim] - width, None, axis...  69.2 us
    all_gather x1, blocking collectives, shards(): arrived = lax.all_gather(wall_flux, 'blk', axis=0, tiled=True)  59.1 us
    all_gather x1, blocking collectives, shards(): lax.all_gather(interface_heat_level, 'blk', axis=0, tiled=True)  49.3 us
    ppermute x18, starting transfers between devices, padded(): lax.ppermute(lax.slice_in_dim(block, 0, width, axis=dim), axis, backward)  30.7 us
    unnamed x1, blocking collectives  26.2 us
    ppermute x18, waiting for transfers between devices, padded(): lax.ppermute(lax.slice_in_dim(block, block.shape[dim] - width, None, axis...  14.4 us
    dot_general x4, matrix products, fluid_operator(): jnp.einsum('fg,gxyz->fxyz', jacobian, centre, precision=lax.Precision.HIG...  9.52 us
  transfers between devices with their start and end apart: 36, of which 14 were waited for; matrix products, arithmetic and copies ran while one was open for 4% of the time, Pallas kernels for 0%

commit v1 on v0

--- a/solution.py
+++ b/solution.py
@@ -148,7 +148,7 @@
     output_entries = jnp.take(boundary_patches_finished, owner_local * rows + target_local, axis=0)
     gas_outcome = adjoint.at[4, 0].add(wall_coefficient[0] * output_entries)
     solid_squares = jnp.sum(metal_imbalance_grid * metal_imbalance_grid)[None]
-    totals = lax.psum(jnp.concatenate([fluid_squares, solid_squares]), ("blk", "span"))
+    totals = lax.psum(lax.psum(jnp.concatenate([fluid_squares, solid_squares]), "blk"), "span")
     every_processor = lax.axis_size("blk") * lax.axis_size("span")
     fluid_cells = float(adjoint.shape[1] * adjoint.shape[2] * adjoint.shape[3] * every_processor)
     solid_cells = float(

time: 372 us -> 380 us (1.022)
  blocking collectives: 224 us -> 230 us
    psum x1 -> x2, blocking collectives: 89.1 us -> 92.9 us  [the longest x1 76.3 us: shards(): lax.psum(jnp.concatenate([fluid_squares, solid_squares]), 'blk')]
  transfers between devices with their start and end apart: 36 -> 36, of which waited for: 14 -> 14; matrix products, arithmetic and copies ran while one was open for 4% -> 3% of each run, Pallas kernels for 0% -> 0%
where the time goes in v1:
time: 380 us; the launch traced here: 377 us
  blocking collectives  230 us (61%)
  starting transfers between devices  99.9 us (26%)
  waiting for transfers between devices  18.5 us (5%)
  matrix products  10.4 us (3%)
  other arithmetic  8.88 us (2%)
  local copies, waits for them, and re-layouts  6.84 us (2%)
    psum x1, blocking collectives, shards(): lax.psum(jnp.concatenate([fluid_squares, solid_squares]), 'blk')  76.3 us
    ppermute x18, starting transfers between devices, padded(): lax.ppermute(lax.slice_in_dim(block, block.shape[dim] - width, None, axis...  69.2 us
    all_gather x1, blocking collectives, shards(): arrived = lax.all_gather(wall_flux, 'blk', axis=0, tiled=True)  59.1 us
    all_gather x1, blocking collectives, shards(): lax.all_gather(interface_heat_level, 'blk', axis=0, tiled=True)  52.2 us
    ppermute x18, starting transfers between devices, padded(): lax.ppermute(lax.slice_in_dim(block, 0, width, axis=dim), axis, backward)  30.7 us
    unnamed x1, blocking collectives  26.2 us
    psum x1, blocking collectives, shards(): lax.psum(lax.psum(jnp.concatenate([fluid_squares, solid_squares]), 'blk')...  16.6 us
    ppermute x18, waiting for transfers between devices, padded(): lax.ppermute(lax.slice_in_dim(block, block.shape[dim] - width, None, axis...  14.5 us
  transfers between devices with their start and end apart: 36, of which 14 were waited for; matrix products, arithmetic and copies ran while one was open for 3% of the time, Pallas kernels for 0%

profile of v1, /device:TPU:2, one launch (start us, length us, event | category | flops | bytes accessed | tf_op | source)
XLA Modules:
  0.0 377.2 jit_solution(12776028832704254321)
XLA Ops:
  3.0 3.4 collective-permute-start.1
  6.4 2.4 collective-permute-start
  9.6 3.4 collective-permute-start.17
  13.0 2.4 collective-permute-start.16
  15.5 3.4 collective-permute-start.21
  20.5 26.2 %all-reduce.11 = (s32[1024]{0:T(1024)S(1)}, s32[1024]{0:T(1024)S(1)}) all-reduce(s32[1024]{0:T(1024)S(1)} %bitcast_dynamic-update-slice_fusion.1, s32[1024]{0:T(1024)S(1)} %bitcast_dynamic-update-slice_fusion), channel_id=2, replica_groups=mesh['blk'=32,'span'=8] {'blk'}, use_global_device_ids=true, to_apply=%add.9 | all-reduce | flops 2048 | bytes 16384
  47.4 2.5 collective-permute-start.20
  51.8 3.0 collective-permute-start.3
  56.2 3.7 collective-permute-start.19
  60.7 2.7 fusion.10
  65.4 3.9 %collective-permute-start.5 = (f32[5,1,32,128]{3,0,2,1:T(8,128)S(1)}, f32[5,1,32,128]{3,0,2,1:T(8,128)S(1)}, u32[]{:S(2)}, u32[]{:S(2)}) collective-permute-start(f32[5,1,32,128]{3,0,2,1:T(8,128)S(1)} %get-tuple-element.56), channel_id=1, source_target_pairs={{0,8},{8,16},{16,24},{24,32},{32,40},{40,48},{48,56},{56,64},{64,7... | collective-permute-start | bytes 245768 | tf_op jit(solution)/shard_map/ppermute | solution.py:16
  71.0 1.9 collective-permute-done.5
  74.2 3.1 collective-permute-start.7
  79.0 2.2 fusion.11
  83.1 4.2 %collective-permute-start.9 = (f32[5,1,32,128]{3,0,2,1:T(8,128)S(1)}, f32[5,1,32,128]{3,0,2,1:T(8,128)S(1)}, u32[]{:S(2)}, u32[]{:S(2)}) collective-permute-start(f32[5,1,32,128]{3,0,2,1:T(8,128)S(1)} %get-tuple-element.54), channel_id=1, source_target_pairs={{0,8},{8,16},{16,24},{24,32},{32,40},{40,48},{48,56},{56,64},{64,7... | collective-permute-start | bytes 245768 | tf_op jit(solution)/shard_map/ppermute | solution.py:16
  91.8 3.4 collective-permute-start.11
  96.5 5.7 %collective-permute-start.23 = (f32[18,1,128]{2,1,0:T(1,128)S(1)}, f32[18,1,128]{2,1,0:T(1,128)S(1)}, u32[]{:S(2)}, u32[]{:S(2)}) collective-permute-start(f32[18,1,128]{2,1,0:T(1,128)S(1)} %get-tuple-element.72), channel_id=1, source_target_pairs={{0,1},{1,2},{2,3},{3,4},{4,5},{5,6},{6,7},{8,9},{9,10},{10,11},{11... | collective-permute-start | bytes 27656 | tf_op jit(solution)/shard_map/ppermute | solution.py:16
  103.0 2.2 fusion.12
  107.2 3.9 %collective-permute-start.13 = (f32[5,1,32,128]{3,0,2,1:T(8,128)S(1)}, f32[5,1,32,128]{3,0,2,1:T(8,128)S(1)}, u32[]{:S(2)}, u32[]{:S(2)}) collective-permute-start(f32[5,1,32,128]{3,0,2,1:T(8,128)S(1)} %get-tuple-element.52), channel_id=1, source_target_pairs={{0,8},{8,16},{16,24},{24,32},{32,40},{40,48},{48,56},{56,64},{64,7... | collective-permute-start | bytes 245768 | tf_op jit(solution)/shard_map/ppermute | solution.py:16
  112.4 2.3 collective-permute-done.13
  116.2 3.1 collective-permute-start.15
  121.0 2.5 multiply_reduce_fusion
  123.5 59.1 %all_gather.14 = f32[1024,128]{1,0:T(8,128)S(1)} all-gather(f32[32,128]{1,0:T(8,128)S(1)} %bitcast_multiply_fusion), channel_id=1, replica_groups=mesh['blk'=32,'span'=8] {'blk'}, dimensions={0}, use_global_device_ids=true | all-gather | bytes 540672 | tf_op jit(solution)/shard_map/all_gather | solution.py:129
  186.0 3.9 %collective-permute-start.25 = (f32[1,32,128]{2,1,0:T(8,128)S(1)}, f32[1,32,128]{2,1,0:T(8,128)S(1)}, u32[]{:S(2)}, u32[]{:S(2)}) collective-permute-start(f32[1,32,128]{2,1,0:T(8,128)S(1)} %get-tuple-element.78), channel_id=1, source_target_pairs={{0,8},{8,16},{16,24},{24,32},{32,40},{40,48},{48,56},{56,64},{64,7... | collective-permute-start | bytes 49160 | tf_op jit(solution)/shard_map/ppermute | solution.py:16
  193.0 3.0 collective-permute-start.27
  199.5 3.9 %collective-permute-start.29 = (f32[1,32,128]{2,1,0:T(8,128)S(1)}, f32[1,32,128]{2,1,0:T(8,128)S(1)}, u32[]{:S(2)}, u32[]{:S(2)}) collective-permute-start(f32[1,32,128]{2,1,0:T(8,128)S(1)} %get-tuple-element.76), channel_id=1, source_target_pairs={{0,8},{8,16},{16,24},{24,32},{32,40},{40,48},{48,56},{56,64},{64,7... | collective-permute-start | bytes 49160 | tf_op jit(solution)/shard_map/ppermute | solution.py:16
  206.4 5.1 %collective-permute-start.31 = (f32[18,1,128]{2,1,0:T(1,128)S(1)}, f32[18,1,128]{2,1,0:T(1,128)S(1)}, u32[]{:S(2)}, u32[]{:S(2)}) collective-permute-start(f32[18,1,128]{2,1,0:T(1,128)S(1)} %get-tuple-element.66), channel_id=1, source_target_pairs={{0,1},{1,2},{2,3},{3,4},{4,5},{5,6},{6,7},{8,9},{9,10},{10,11},{11... | collective-permute-start | bytes 27656 | tf_op jit(solution)/shard_map/ppermute | solution.py:16
  215.0 4.2 %collective-permute-start.33 = (f32[1,32,128]{2,1,0:T(8,128)S(1)}, f32[1,32,128]{2,1,0:T(8,128)S(1)}, u32[]{:S(2)}, u32[]{:S(2)}) collective-permute-start(f32[1,32,128]{2,1,0:T(8,128)S(1)} %get-tuple-element.74), channel_id=1, source_target_pairs={{0,8},{8,16},{16,24},{24,32},{32,40},{40,48},{48,56},{56,64},{64,7... | collective-permute-start | bytes 49160 | tf_op jit(solution)/shard_map/ppermute | solution.py:16
  222.0 4.8 %collective-permute-start.35 = (f32[18,1,128]{2,1,0:T(1,128)S(1)}, f32[18,1,128]{2,1,0:T(1,128)S(1)}, u32[]{:S(2)}, u32[]{:S(2)}) collective-permute-start(f32[18,1,128]{2,1,0:T(1,128)S(1)} %get-tuple-element.64), channel_id=1, source_target_pairs={{0,1},{1,2},{2,3},{3,4},{4,5},{5,6},{6,7},{8,9},{9,10},{10,11},{11... | collective-permute-start | bytes 27656 | tf_op jit(solution)/shard_map/ppermute | solution.py:16
  229.6 76.3 %psum.14 = f32[6]{0:T(128)S(1)} all-reduce(f32[6]{0:T(128)S(1)} %pad_maximum_fusion.78), channel_id=1, replica_groups=mesh['blk'=32,'span'=8] {'blk'}, use_global_device_ids=true, to_apply=%region_2.3 | all-reduce | flops 6 | bytes 48 | tf_op jit(solution)/shard_map/psum | solution.py:151
  305.9 16.6 %psum.15 = f32[6]{0:T(128)S(1)} all-reduce(f32[6]{0:T(128)S(1)} %psum.14), channel_id=1, replica_groups=mesh['blk'=32,'span'=8] {'span'}, use_global_device_ids=true, to_apply=%region_3.4 | all-reduce | flops 6 | bytes 48 | tf_op jit(solution)/shard_map/psum | solution.py:151
  322.8 52.2 %all-gather.2 = f32[1,1024,128]{2,1,0:T(8,128)S(1)} all-gather(f32[1,32,128]{2,1,0:T(8,128)S(1)} %slice.616), channel_id=4, replica_groups=mesh['blk'=32,'span'=8] {'blk'}, dimensions={1}, use_global_device_ids=true | all-gather | bytes 540672 | tf_op jit(solution)/shard_map/all_gather | solution.py:147
  (154 shorter events, 54.2 us)
Async XLA Ops:
  3.0 46.9 %collective-permute-start.1 = (f32[5,1,32,128]{3,0,2,1:T(8,128)}, f32[5,1,32,128]{3,0,2,1:T(8,128)S(1)}, u32[]{:S(2)}, u32[]{:S(2)}) collective-permute-start(f32[5,1,32,128]{3,0,2,1:T(8,128)} %get-tuple-element.59), channel_id=1, source_target_pairs={{0,8},{8,16},{16,24},{24,32},{32,40},{40,48},{48,56},{56,64},{64,7... | collective-permute-start | bytes 245768 | tf_op jit(solution)/shard_map/ppermute | solution.py:16
  6.4 44.0 %collective-permute-start = (f32[5,1,32,128]{3,0,2,1:T(8,128)}, f32[5,1,32,128]{3,0,2,1:T(8,128)S(1)}, u32[]{:S(2)}, u32[]{:S(2)}) collective-permute-start(f32[5,1,32,128]{3,0,2,1:T(8,128)} %get-tuple-element.58), channel_id=1, source_target_pairs={{8,0},{16,8},{24,16},{32,24},{40,32},{48,40},{56,48},{64,56},{72,6... | collective-permute-start | bytes 245768 | tf_op jit(solution)/shard_map/ppermute | solution.py:19
  9.6 37.7 %collective-permute-start.17 = (f32[1,32,128]{2,1,0:T(8,128)S(1)}, f32[1,32,128]{2,1,0:T(8,128)S(1)}, u32[]{:S(2)}, u32[]{:S(2)}) collective-permute-start(f32[1,32,128]{2,1,0:T(8,128)S(1)} %get-tuple-element.80), channel_id=1, source_target_pairs={{0,8},{8,16},{16,24},{24,32},{32,40},{40,48},{48,56},{56,64},{64,7... | collective-permute-start | bytes 49160 | tf_op jit(solution)/shard_map/ppermute | solution.py:16
  13.0 36.9 %collective-permute-start.16 = (f32[1,32,128]{2,1,0:T(8,128)S(1)}, f32[1,32,128]{2,1,0:T(8,128)S(1)}, u32[]{:S(2)}, u32[]{:S(2)}) collective-permute-start(f32[1,32,128]{2,1,0:T(8,128)S(1)} %get-tuple-element.81), channel_id=1, source_target_pairs={{8,0},{16,8},{24,16},{32,24},{40,32},{48,40},{56,48},{64,56},{72,6... | collective-permute-start | bytes 49160 | tf_op jit(solution)/shard_map/ppermute | solution.py:19
  15.5 49.9 %collective-permute-start.21 = (f32[1,32,128]{2,1,0:T(8,128)S(1)}, f32[1,32,128]{2,1,0:T(8,128)S(1)}, u32[]{:S(2)}, u32[]{:S(2)}) collective-permute-start(f32[1,32,128]{2,1,0:T(8,128)S(1)} %get-tuple-element.83), channel_id=1, source_target_pairs={{0,8},{8,16},{16,24},{24,32},{32,40},{40,48},{48,56},{56,64},{64,7... | collective-permute-start | bytes 49160 | tf_op jit(solution)/shard_map/ppermute | solution.py:16
  47.4 39.9 %collective-permute-start.20 = (f32[1,32,128]{2,1,0:T(8,128)S(1)}, f32[1,32,128]{2,1,0:T(8,128)S(1)}, u32[]{:S(2)}, u32[]{:S(2)}) collective-permute-start(f32[1,32,128]{2,1,0:T(8,128)S(1)} %get-tuple-element.82), channel_id=1, source_target_pairs={{8,0},{16,8},{24,16},{32,24},{40,32},{48,40},{56,48},{64,56},{72,6... | collective-permute-start | bytes 49160 | tf_op jit(solution)/shard_map/ppermute | solution.py:19
  50.5 5.7 %collective-permute-start.2 = (f32[5,10,1,128]{3,0,2,1:T(8,128)S(1)}, f32[5,10,1,128]{3,0,2,1:T(8,128)S(1)}, u32[]{:S(2)}, u32[]{:S(2)}) collective-permute-start(f32[5,10,1,128]{3,0,2,1:T(8,128)S(1)} %get-tuple-element.49), channel_id=1, source_target_pairs={{1,0},{2,1},{3,2},{4,3},{5,4},{6,5},{7,6},{9,8},{10,9},{11,10},{12... | collective-permute-start | bytes 76808 | tf_op jit(solution)/shard_map/ppermute | solution.py:19
  51.8 8.1 %collective-permute-start.3 = (f32[5,10,1,128]{3,0,2,1:T(8,128)S(1)}, f32[5,10,1,128]{3,0,2,1:T(8,128)S(1)}, u32[]{:S(2)}, u32[]{:S(2)}) collective-permute-start(f32[5,10,1,128]{3,0,2,1:T(8,128)S(1)} %get-tuple-element.48), channel_id=1, source_target_pairs={{0,1},{1,2},{2,3},{3,4},{4,5},{5,6},{6,7},{8,9},{9,10},{10,11},{11... | collective-permute-start | bytes 76808 | tf_op jit(solution)/shard_map/ppermute | solution.py:16
  54.8 52.3 %collective-permute-start.18 = (f32[18,1,128]{2,1,0:T(1,128)S(1)}, f32[18,1,128]{2,1,0:T(1,128)S(1)}, u32[]{:S(2)}, u32[]{:S(2)}) collective-permute-start(f32[18,1,128]{2,1,0:T(1,128)S(1)} %get-tuple-element.71), channel_id=1, source_target_pairs={{1,0},{2,1},{3,2},{4,3},{5,4},{6,5},{7,6},{9,8},{10,9},{11,10},{12... | collective-permute-start | bytes 27656 | tf_op jit(solution)/shard_map/ppermute | solution.py:19
  56.2 54.9 %collective-permute-start.19 = (f32[18,1,128]{2,1,0:T(1,128)S(1)}, f32[18,1,128]{2,1,0:T(1,128)S(1)}, u32[]{:S(2)}, u32[]{:S(2)}) collective-permute-start(f32[18,1,128]{2,1,0:T(1,128)S(1)} %get-tuple-element.70), channel_id=1, source_target_pairs={{0,1},{1,2},{2,3},{3,4},{4,5},{5,6},{6,7},{8,9},{9,10},{10,11},{11... | collective-permute-start | bytes 27656 | tf_op jit(solution)/shard_map/ppermute | solution.py:16
  63.4 7.5 %collective-permute-start.4 = (f32[5,1,32,128]{3,0,2,1:T(8,128)S(1)}, f32[5,1,32,128]{3,0,2,1:T(8,128)S(1)}, u32[]{:S(2)}, u32[]{:S(2)}) collective-permute-start(f32[5,1,32,128]{3,0,2,1:T(8,128)S(1)} %get-tuple-element.57), channel_id=1, source_target_pairs={{8,0},{16,8},{24,16},{32,24},{40,32},{48,40},{56,48},{64,56},{72,6... | collective-permute-start | bytes 245768 | tf_op jit(solution)/shard_map/ppermute | solution.py:19
  65.4 7.5 %collective-permute-start.5 = (f32[5,1,32,128]{3,0,2,1:T(8,128)S(1)}, f32[5,1,32,128]{3,0,2,1:T(8,128)S(1)}, u32[]{:S(2)}, u32[]{:S(2)}) collective-permute-start(f32[5,1,32,128]{3,0,2,1:T(8,128)S(1)} %get-tuple-element.56), channel_id=1, source_target_pairs={{0,8},{8,16},{16,24},{24,32},{32,40},{40,48},{48,56},{56,64},{64,7... | collective-permute-start | bytes 245768 | tf_op jit(solution)/shard_map/ppermute | solution.py:16
  72.9 4.4 %collective-permute-start.6 = (f32[5,10,1,128]{3,0,2,1:T(8,128)S(1)}, f32[5,10,1,128]{3,0,2,1:T(8,128)S(1)}, u32[]{:S(2)}, u32[]{:S(2)}) collective-permute-start(f32[5,10,1,128]{3,0,2,1:T(8,128)S(1)} %get-tuple-element.47), channel_id=1, source_target_pairs={{1,0},{2,1},{3,2},{4,3},{5,4},{6,5},{7,6},{9,8},{10,9},{11,10},{12... | collective-permute-start | bytes 76808 | tf_op jit(solution)/shard_map/ppermute | solution.py:19
  81.2 7.5 %collective-permute-start.8 = (f32[5,1,32,128]{3,0,2,1:T(8,128)S(1)}, f32[5,1,32,128]{3,0,2,1:T(8,128)S(1)}, u32[]{:S(2)}, u32[]{:S(2)}) collective-permute-start(f32[5,1,32,128]{3,0,2,1:T(8,128)S(1)} %get-tuple-element.55), channel_id=1, source_target_pairs={{8,0},{16,8},{24,16},{32,24},{40,32},{48,40},{56,48},{64,56},{72,6... | collective-permute-start | bytes 245768 | tf_op jit(solution)/shard_map/ppermute | solution.py:19
  83.1 7.4 %collective-permute-start.9 = (f32[5,1,32,128]{3,0,2,1:T(8,128)S(1)}, f32[5,1,32,128]{3,0,2,1:T(8,128)S(1)}, u32[]{:S(2)}, u32[]{:S(2)}) collective-permute-start(f32[5,1,32,128]{3,0,2,1:T(8,128)S(1)} %get-tuple-element.54), channel_id=1, source_target_pairs={{0,8},{8,16},{16,24},{24,32},{32,40},{40,48},{48,56},{56,64},{64,7... | collective-permute-start | bytes 245768 | tf_op jit(solution)/shard_map/ppermute | solution.py:16
  90.5 6.0 %collective-permute-start.10 = (f32[5,10,1,128]{3,0,2,1:T(8,128)S(1)}, f32[5,10,1,128]{3,0,2,1:T(8,128)S(1)}, u32[]{:S(2)}, u32[]{:S(2)}) collective-permute-start(f32[5,10,1,128]{3,0,2,1:T(8,128)S(1)} %get-tuple-element.45), channel_id=1, source_target_pairs={{1,0},{2,1},{3,2},{4,3},{5,4},{6,5},{7,6},{9,8},{10,9},{11,10},{12... | collective-permute-start | bytes 76808 | tf_op jit(solution)/shard_map/ppermute | solution.py:19
  91.8 10.4 %collective-permute-start.11 = (f32[5,10,1,128]{3,0,2,1:T(8,128)S(1)}, f32[5,10,1,128]{3,0,2,1:T(8,128)S(1)}, u32[]{:S(2)}, u32[]{:S(2)}) collective-permute-start(f32[5,10,1,128]{3,0,2,1:T(8,128)S(1)} %get-tuple-element.44), channel_id=1, source_target_pairs={{0,1},{1,2},{2,3},{3,4},{4,5},{5,6},{6,7},{8,9},{9,10},{10,11},{11... | collective-permute-start | bytes 76808 | tf_op jit(solution)/shard_map/ppermute | solution.py:16
  95.2 24.1 %collective-permute-start.22 = (f32[18,1,128]{2,1,0:T(1,128)S(1)}, f32[18,1,128]{2,1,0:T(1,128)S(1)}, u32[]{:S(2)}, u32[]{:S(2)}) collective-permute-start(f32[18,1,128]{2,1,0:T(1,128)S(1)} %get-tuple-element.73), channel_id=1, source_target_pairs={{1,0},{2,1},{3,2},{4,3},{5,4},{6,5},{7,6},{9,8},{10,9},{11,10},{12... | collective-permute-start | bytes 27656 | tf_op jit(solution)/shard_map/ppermute | solution.py:19
  96.5 22.8 %collective-permute-start.23 = (f32[18,1,128]{2,1,0:T(1,128)S(1)}, f32[18,1,128]{2,1,0:T(1,128)S(1)}, u32[]{:S(2)}, u32[]{:S(2)}) collective-permute-start(f32[18,1,128]{2,1,0:T(1,128)S(1)} %get-tuple-element.72), channel_id=1, source_target_pairs={{0,1},{1,2},{2,3},{3,4},{4,5},{5,6},{6,7},{8,9},{9,10},{10,11},{11... | collective-permute-start | bytes 27656 | tf_op jit(solution)/shard_map/ppermute | solution.py:16
  105.2 7.2 %collective-permute-start.12 = (f32[5,1,32,128]{3,0,2,1:T(8,128)S(1)}, f32[5,1,32,128]{3,0,2,1:T(8,128)S(1)}, u32[]{:S(2)}, u32[]{:S(2)}) collective-permute-start(f32[5,1,32,128]{3,0,2,1:T(8,128)S(1)} %get-tuple-element.53), channel_id=1, source_target_pairs={{8,0},{16,8},{24,16},{32,24},{40,32},{48,40},{56,48},{64,56},{72,6... | collective-permute-start | bytes 245768 | tf_op jit(solution)/shard_map/ppermute | solution.py:19
  107.2 7.5 %collective-permute-start.13 = (f32[5,1,32,128]{3,0,2,1:T(8,128)S(1)}, f32[5,1,32,128]{3,0,2,1:T(8,128)S(1)}, u32[]{:S(2)}, u32[]{:S(2)}) collective-permute-start(f32[5,1,32,128]{3,0,2,1:T(8,128)S(1)} %get-tuple-element.52), channel_id=1, source_target_pairs={{0,8},{8,16},{16,24},{24,32},{32,40},{40,48},{48,56},{56,64},{64,7... | collective-permute-start | bytes 245768 | tf_op jit(solution)/shard_map/ppermute | solution.py:16
  114.7 4.9 %collective-permute-start.14 = (f32[5,10,1,128]{3,0,2,1:T(8,128)S(1)}, f32[5,10,1,128]{3,0,2,1:T(8,128)S(1)}, u32[]{:S(2)}, u32[]{:S(2)}) collective-permute-start(f32[5,10,1,128]{3,0,2,1:T(8,128)S(1)} %get-tuple-element.43), channel_id=1, source_target_pairs={{1,0},{2,1},{3,2},{4,3},{5,4},{6,5},{7,6},{9,8},{10,9},{11,10},{12... | collective-permute-start | bytes 76808 | tf_op jit(solution)/shard_map/ppermute | solution.py:19
  184.1 5.9 %collective-permute-start.24 = (f32[1,32,128]{2,1,0:T(8,128)S(1)}, f32[1,32,128]{2,1,0:T(8,128)S(1)}, u32[]{:S(2)}, u32[]{:S(2)}) collective-permute-start(f32[1,32,128]{2,1,0:T(8,128)S(1)} %get-tuple-element.79), channel_id=1, source_target_pairs={{8,0},{16,8},{24,16},{32,24},{40,32},{48,40},{56,48},{64,56},{72,6... | collective-permute-start | bytes 49160 | tf_op jit(solution)/shard_map/ppermute | solution.py:19
  186.0 5.6 %collective-permute-start.25 = (f32[1,32,128]{2,1,0:T(8,128)S(1)}, f32[1,32,128]{2,1,0:T(8,128)S(1)}, u32[]{:S(2)}, u32[]{:S(2)}) collective-permute-start(f32[1,32,128]{2,1,0:T(8,128)S(1)} %get-tuple-element.78), channel_id=1, source_target_pairs={{0,8},{8,16},{16,24},{24,32},{32,40},{40,48},{48,56},{56,64},{64,7... | collective-permute-start | bytes 49160 | tf_op jit(solution)/shard_map/ppermute | solution.py:16
  197.5 5.9 %collective-permute-start.28 = (f32[1,32,128]{2,1,0:T(8,128)S(1)}, f32[1,32,128]{2,1,0:T(8,128)S(1)}, u32[]{:S(2)}, u32[]{:S(2)}) collective-permute-start(f32[1,32,128]{2,1,0:T(8,128)S(1)} %get-tuple-element.77), channel_id=1, source_target_pairs={{8,0},{16,8},{24,16},{32,24},{40,32},{48,40},{56,48},{64,56},{72,6... | collective-permute-start | bytes 49160 | tf_op jit(solution)/shard_map/ppermute | solution.py:19
  199.5 5.6 %collective-permute-start.29 = (f32[1,32,128]{2,1,0:T(8,128)S(1)}, f32[1,32,128]{2,1,0:T(8,128)S(1)}, u32[]{:S(2)}, u32[]{:S(2)}) collective-permute-start(f32[1,32,128]{2,1,0:T(8,128)S(1)} %get-tuple-element.76), channel_id=1, source_target_pairs={{0,8},{8,16},{16,24},{24,32},{32,40},{40,48},{48,56},{56,64},{64,7... | collective-permute-start | bytes 49160 | tf_op jit(solution)/shard_map/ppermute | solution.py:16
  205.1 6.4 %collective-permute-start.30 = (f32[18,1,128]{2,1,0:T(1,128)S(1)}, f32[18,1,128]{2,1,0:T(1,128)S(1)}, u32[]{:S(2)}, u32[]{:S(2)}) collective-permute-start(f32[18,1,128]{2,1,0:T(1,128)S(1)} %get-tuple-element.67), channel_id=1, source_target_pairs={{1,0},{2,1},{3,2},{4,3},{5,4},{6,5},{7,6},{9,8},{10,9},{11,10},{12... | collective-permute-start | bytes 27656 | tf_op jit(solution)/shard_map/ppermute | solution.py:19
  206.4 5.9 %collective-permute-start.31 = (f32[18,1,128]{2,1,0:T(1,128)S(1)}, f32[18,1,128]{2,1,0:T(1,128)S(1)}, u32[]{:S(2)}, u32[]{:S(2)}) collective-permute-start(f32[18,1,128]{2,1,0:T(1,128)S(1)} %get-tuple-element.66), channel_id=1, source_target_pairs={{0,1},{1,2},{2,3},{3,4},{4,5},{5,6},{6,7},{8,9},{9,10},{10,11},{11... | collective-permute-start | bytes 27656 | tf_op jit(solution)/shard_map/ppermute | solution.py:16
  213.1 6.2 %collective-permute-start.32 = (f32[1,32,128]{2,1,0:T(8,128)S(1)}, f32[1,32,128]{2,1,0:T(8,128)S(1)}, u32[]{:S(2)}, u32[]{:S(2)}) collective-permute-start(f32[1,32,128]{2,1,0:T(8,128)S(1)} %get-tuple-element.75), channel_id=1, source_target_pairs={{8,0},{16,8},{24,16},{32,24},{40,32},{48,40},{56,48},{64,56},{72,6... | collective-permute-start | bytes 49160 | tf_op jit(solution)/shard_map/ppermute | solution.py:19
  215.0 5.6 %collective-permute-start.33 = (f32[1,32,128]{2,1,0:T(8,128)S(1)}, f32[1,32,128]{2,1,0:T(8,128)S(1)}, u32[]{:S(2)}, u32[]{:S(2)}) collective-permute-start(f32[1,32,128]{2,1,0:T(8,128)S(1)} %get-tuple-element.74), channel_id=1, source_target_pairs={{0,8},{8,16},{16,24},{24,32},{32,40},{40,48},{48,56},{56,64},{64,7... | collective-permute-start | bytes 49160 | tf_op jit(solution)/shard_map/ppermute | solution.py:16
  220.7 6.1 %collective-permute-start.34 = (f32[18,1,128]{2,1,0:T(1,128)S(1)}, f32[18,1,128]{2,1,0:T(1,128)S(1)}, u32[]{:S(2)}, u32[]{:S(2)}) collective-permute-start(f32[18,1,128]{2,1,0:T(1,128)S(1)} %get-tuple-element.65), channel_id=1, source_target_pairs={{1,0},{2,1},{3,2},{4,3},{5,4},{6,5},{7,6},{9,8},{10,9},{11,10},{12... | collective-permute-start | bytes 27656 | tf_op jit(solution)/shard_map/ppermute | solution.py:19
  222.0 5.6 %collective-permute-start.35 = (f32[18,1,128]{2,1,0:T(1,128)S(1)}, f32[18,1,128]{2,1,0:T(1,128)S(1)}, u32[]{:S(2)}, u32[]{:S(2)}) collective-permute-start(f32[18,1,128]{2,1,0:T(1,128)S(1)} %get-tuple-element.64), channel_id=1, source_target_pairs={{0,1},{1,2},{2,3},{3,4},{4,5},{5,6},{6,7},{8,9},{9,10},{10,11},{11... | collective-permute-start | bytes 27656 | tf_op jit(solution)/shard_map/ppermute | solution.py:16
  (24 other events, 817.7 us)
